TPU v7x, 256 devices: a whole 4x4x8 slice. The times are simulated.
256 devices in a mesh: trow: 16 (over x, y), tcol: 8 (over z), rep: 2 (over core).
Axes of the slice: x: 4, y: 4, z: 8, core: 2. Of those that a mesh axis runs over, the one named last changes fastest.
Arguments:
- users: float32 [131072, 128], P(('trow', 'tcol'))
- items: float32 [65536, 128], P(('tcol', 'trow'))
- ratings: bfloat16 [16, 8, 2, 64, 128, 128], P('trow', 'tcol', 'rep'), may hold values from -6 to 6
- row_mask: int32 [16, 8, 2, 64, 128], P('trow', 'tcol', 'rep'), may hold values 0 or 1
- col_mask: int32 [16, 8, 2, 64, 128], P('trow', 'tcol', 'rep'), may hold values 0 or 1
- row_slots: int32 [16, 8, 2, 64], P('trow', 'tcol', 'rep'), may hold values from 0 to 31, as said below
- col_slots: int32 [16, 8, 2, 64], P('trow', 'tcol', 'rep'), may hold values from 0 to 31, as said below
- send_users: int32 [16, 8, 2, 8, 4], P('trow', 'tcol', 'rep'), may hold values from 0 to 7, as said below
- send_items: int32 [16, 8, 2, 16, 2], P('trow', 'tcol', 'rep'), may hold values from 0 to 3, as said below
Outputs:
- users_out: float32 [131072, 128], P(('trow', 'tcol'))
- items_out: float32 [65536, 128], P(('tcol', 'trow'))
Inputs may be any that keep to these rules, and one draw needn't show every extreme that they name: `send_users`: distinct within each row of the last dimension. `send_items`: distinct within each row of the last dimension. `row_slots`: every slot is named by some tile of each device. `col_slots`: every slot is named by some tile of each device.
All inputs are finite; a program needn't handle non-finite values. No bound on the sum of `row_mask` or of `col_mask` on one device may be relied on, other than what follows from the above.
Results may differ from a plain program's by a relative error of at most 0.02.
Values may be sent and summed in bfloat16 or wider, within the bound.
A program may use at most 64 MiB of HBM per device.

v0:
```python
import jax
import jax.numpy as jnp
from jax import lax
from jax.sharding import PartitionSpec as P

ITERS = 2


def precondition(gradient, gramian):
    factor = jnp.linalg.cholesky(gramian)
    return jax.scipy.linalg.cho_solve((factor, True), gradient.T).T


def pool_sum(index_list, terms, pool_count):
    onehot = (
        lax.broadcasted_iota(jnp.int32, (pool_count, index_list.shape[0]), 0) == index_list[None, :]
    ).astype(jnp.bfloat16)
    flat = terms.reshape(terms.shape[0], -1)
    upper = flat.astype(jnp.bfloat16)
    lower = (flat - upper.astype(jnp.float32)).astype(jnp.bfloat16)
    return jnp.dot(onehot, upper, preferred_element_type=jnp.float32) + jnp.dot(
        onehot, lower, preferred_element_type=jnp.float32
    )


def on_device(
    users, items, ratings, row_mask, col_mask, row_slots, col_slots, send_users, send_items
):
    n_trow = lax.axis_size("trow")
    n_tcol = lax.axis_size("tcol")
    n_rep = lax.axis_size("rep")
    tile_size = ratings.shape[-1]
    rank_width = users.shape[1]
    tile_count = ratings.shape[3]
    own_users = users.shape[0] // tile_size
    own_items = items.shape[0] // tile_size
    user_cap = send_users.shape[-1]
    item_cap = send_items.shape[-1]
    ratings_local = ratings.reshape(tile_count, tile_size, tile_size)
    weights = (
        row_mask.reshape(tile_count, tile_size)[:, :, None]
        * col_mask.reshape(tile_count, tile_size)[:, None, :]
    ).astype(jnp.float32)
    row_slot_list = row_slots.reshape(-1)
    col_slot_list = col_slots.reshape(-1)
    user_sends = send_users.reshape(n_tcol, -1)
    item_sends = send_items.reshape(n_trow, -1)
    user_received = lax.all_to_all(
        user_sends, "tcol", split_axis=0, concat_axis=0, tiled=True
    ).reshape(-1)
    item_received = lax.all_to_all(
        item_sends, "trow", split_axis=0, concat_axis=0, tiled=True
    ).reshape(-1)
    row_list = row_slot_list // user_cap * own_users + user_received[row_slot_list]
    col_list = col_slot_list // item_cap * own_items + item_received[col_slot_list]
    all_users = own_users * tile_size * n_trow * n_tcol
    all_items = own_items * tile_size * n_trow * n_tcol
    user_coef = 2.0 * all_items * own_users / (tile_size * tile_count * n_rep)
    item_coef = 2.0 * all_users * own_items / (tile_size * tile_count * n_rep)
    for iteration in range(ITERS):
        gram_users, gram_items = lax.psum(
            (
                jnp.dot(
                    users.T,
                    users,
                    precision=lax.Precision.HIGHEST,
                    preferred_element_type=jnp.float32,
                ),
                jnp.dot(
                    items.T,
                    items,
                    precision=lax.Precision.HIGHEST,
                    preferred_element_type=jnp.float32,
                ),
            ),
            ("trow", "tcol"),
        )
        user_half = users.astype(jnp.bfloat16).reshape(own_users, tile_size, rank_width)
        item_half = items.astype(jnp.bfloat16).reshape(own_items, tile_size, rank_width)
        user_pool = lax.all_gather(user_half, "tcol", axis=0, tiled=True)
        item_pool = lax.all_gather(item_half, "trow", axis=0, tiled=True)
        x_tiles = user_pool[row_list]
        y_tiles = item_pool[col_list]
        predicted = jnp.einsum("tar,tbr->tab", x_tiles, y_tiles, preferred_element_type=jnp.float32)
        errors = (weights * (predicted - ratings_local.astype(jnp.float32))).astype(jnp.bfloat16)
        user_terms = jnp.einsum("tab,tbr->tar", errors, y_tiles, preferred_element_type=jnp.float32)
        item_terms = jnp.einsum("tab,tar->tbr", errors, x_tiles, preferred_element_type=jnp.float32)
        user_pooled = pool_sum(row_list, user_terms, user_pool.shape[0])
        item_pooled = pool_sum(col_list, item_terms, item_pool.shape[0])
        user_grad = lax.psum_scatter(user_pooled, "tcol", scatter_dimension=0, tiled=True)
        item_grad = lax.psum_scatter(item_pooled, "trow", scatter_dimension=0, tiled=True)
        user_grad, item_grad = lax.psum((user_grad, item_grad), "rep")
        new_users = users - user_coef * precondition(user_grad.reshape(-1, rank_width), gram_items)
        new_items = items - item_coef * precondition(item_grad.reshape(-1, rank_width), gram_users)
        users, items = (new_users, new_items)
    return (users, items)


def solution(mesh):
    return jax.shard_map(
        on_device,
        mesh=mesh,
        in_specs=(
            P(("trow", "tcol"), None),
            P(("tcol", "trow"), None),
            P("trow", "tcol", "rep", None, None, None),
            P("trow", "tcol", "rep", None, None),
            P("trow", "tcol", "rep", None, None),
            P("trow", "tcol", "rep", None),
            P("trow", "tcol", "rep", None),
            P("trow", "tcol", "rep", None, None),
            P("trow", "tcol", "rep", None, None),
        ),
        out_specs=(P(("trow", "tcol"), None), P(("tcol", "trow"), None)),
        check_vma=False,
    )
```

profile of v0, /device:TPU:1, one launch (start us, length us, event | category | flops | bytes accessed | tf_op | source)
XLA Modules:
  0.0 1075.5 jit_solution(2654260133140196737)
XLA Ops:
  7.2 1.8 convert_element_type.69
  9.1 1.6 convert_element_type.70
  10.7 1.3 copy.48
  12.1 7.6 all-to-all-start.1
  21.0 1.3 copy.47
  22.3 3.7 all-to-all-done.1
  26.1 8.2 all-to-all-start
  36.4 4.4 all-to-all-done
  42.3 9.4 all-gather.5.cloned.1.call-done
  51.7 3.7 gather_fusion.1
  55.4 50.8 %all-gather.7.cloned.1.call-done = bf16[64,128,128]{2,1,0:T(8,128)(2,1)} async-done(((bf16[4,128,128]{2,1,0:T(8,128)(2,1)}), bf16[64,128,128]{2,1,0:T(8,128)(2,1)}) %all-gather.7.cloned.1.call-update) | async-done | bytes 2097168 | tf_op jit(solution)/shard_map/all_gather | solution.py:81
  106.3 2.5 gather_fusion.3
  108.9 4.1 fusion.1
  113.0 0.9 fusion.61
  114.4 2.8 fusion.9
  117.2 4.9 convolution_add_fusion.2
  122.3 2.3 fusion.59
  124.6 2.8 fusion.8
  127.4 4.9 convolution_add_fusion.3
  132.4 0.9 copy-done.5
  133.2 1.2 fusion.58
  134.5 1.6 fusion.60
  137.4 98.5 %all-reduce.13.cloned.1.call-done = f32[64,16384]{1,0:T(8,128)} async-done(((f32[64,16384]{1,0:T(8,128)}), f32[64,16384]{1,0:T(8,128)}) %all-reduce.13.cloned.1.call-update) | async-done | bytes 4194320
  235.9 1.1 constant_dynamic-slice_fusion.1
  237.0 0.9 reshape.383
  237.9 55.8 %reduce-scatter.3.cloned.1.call-done = f32[8,16384]{1,0:T(8,128)} async-done(((f32[64,16384]{1,0:T(8,128)}), f32[8,16384]{1,0:T(8,128)}) %reduce-scatter.3.cloned.1.call-update) | async-done | bytes 524304 | tf_op jit(solution)/shard_map/reduce_scatter | solution.py:90
  293.7 1.9 reshape.380
  296.1 209.1 %all-reduce.19.cloned.1.call-done = (f32[128,128]{0,1:T(8,128)}, f32[128,128]{0,1:T(8,128)}) async-done(((f32[128,128]{0,1:T(8,128)}, f32[128,128]{0,1:T(8,128)}), (f32[128,128]{0,1:T(8,128)}, f32[128,128]{0,1:T(8,128)})) %all-reduce.19.cloned.1.call-update) | async-done | bytes 131088 | tf_op jit(solution)/shard_map/psum | solution.py:61
  505.3 0.9 copy.51
  506.2 0.9 copy.46
  507.1 0.9 fusion.39
  508.0 11.7 %cholesky.74 = f32[128,128]{1,0:T(8,128)S(1)} custom-call(f32[128,128]{1,0:T(8,128)S(1)} %get-tuple-element.24), custom_call_target="Cholesky" | custom-call | tf_op jit(solution)/shard_map/jit(cholesky)/cholesky | solution.py:10
  521.1 9.8 custom-call.14
  530.9 10.3 all-reduce.23.cloned.1.call-done
  541.2 1.7 fusion.41
  545.1 11.7 %cholesky.85 = f32[128,128]{1,0:T(8,128)S(1)} custom-call(f32[128,128]{1,0:T(8,128)S(1)} %get-tuple-element.23), custom_call_target="Cholesky" | custom-call | tf_op jit(solution)/shard_map/jit(cholesky)/cholesky | solution.py:10
  558.1 9.8 custom-call.15
  569.6 1.0 fusion.62
  570.6 1.2 fusion.64
  572.0 10.9 %all-gather.9.cloned.1.call-done = bf16[64,128,128]{2,1,0:T(8,128)(2,1)} async-done(((bf16[8,128,128]{2,1,0:T(8,128)(2,1)}), bf16[64,128,128]{2,1,0:T(8,128)(2,1)}) %all-gather.9.cloned.1.call-update) | async-done | bytes 2097168 | tf_op jit(solution)/shard_map/all_gather | solution.py:80
  582.9 3.7 gather_fusion.4
  586.7 50.5 %all-gather.11.cloned.1.call-done = bf16[64,128,128]{2,1,0:T(8,128)(2,1)} async-done(((bf16[4,128,128]{2,1,0:T(8,128)(2,1)}), bf16[64,128,128]{2,1,0:T(8,128)(2,1)}) %all-gather.11.cloned.1.call-update) | async-done | bytes 2097168 | tf_op jit(solution)/shard_map/all_gather | solution.py:81
  637.2 2.5 gather_fusion.5
  639.7 4.1 fusion.3
  643.9 0.9 fusion.65
  645.2 2.8 fusion.11
  648.0 4.9 convolution_add_fusion
  653.0 2.3 fusion.63
  655.3 2.8 fusion.10
  658.1 4.9 convolution_add_fusion.1
  663.2 187.3 %all-reduce.17.cloned.1.call-done = (f32[128,128]{0,1:T(8,128)}, f32[128,128]{0,1:T(8,128)}) async-done(((f32[128,128]{0,1:T(8,128)}, f32[128,128]{0,1:T(8,128)}), (f32[128,128]{0,1:T(8,128)}, f32[128,128]{0,1:T(8,128)})) %all-reduce.17.cloned.1.call-update) | async-done | bytes 131088 | tf_op jit(solution)/shard_map/psum | solution.py:61
  850.6 1.0 copy.55
  851.5 0.9 fusion.35
  852.4 11.7 %cholesky.96 = f32[128,128]{1,0:T(8,128)S(1)} custom-call(f32[128,128]{1,0:T(8,128)S(1)} %fusion.35), custom_call_target="Cholesky" | custom-call | tf_op jit(solution)/shard_map/jit(cholesky)/cholesky | solution.py:10
  864.8 104.5 %all-reduce.15.cloned.1.call-done = f32[64,16384]{1,0:T(8,128)} async-done(((f32[64,16384]{1,0:T(8,128)}), f32[64,16384]{1,0:T(8,128)}) %all-reduce.15.cloned.1.call-update) | async-done | bytes 4194320
  969.4 1.1 constant_dynamic-slice_fusion
  970.5 0.9 reshape.389
  971.4 56.1 %reduce-scatter.5.cloned.1.call-done = f32[8,16384]{1,0:T(8,128)} async-done(((f32[64,16384]{1,0:T(8,128)}), f32[8,16384]{1,0:T(8,128)}) %reduce-scatter.5.cloned.1.call-update) | async-done | bytes 524304 | tf_op jit(solution)/shard_map/reduce_scatter | solution.py:90
  1027.5 1.9 reshape.387
  1030.1 9.8 custom-call.16
  1040.0 11.7 %cholesky.107 = f32[128,128]{1,0:T(8,128)S(1)} custom-call(f32[128,128]{1,0:T(8,128)S(1)} %fusion.31), custom_call_target="Cholesky" | custom-call | tf_op jit(solution)/shard_map/jit(cholesky)/cholesky | solution.py:10
  1053.2 10.0 custom-call.17
  1063.3 1.7 fusion.33
  1065.6 1.0 copy.61
  (95 shorter events, 19.6 us)
Async XLA Ops:
  7.2 35.1 %copy-start.12 = (s32[1,1,1,64]{3,2,1,0:T(1,128)S(1)}, s32[1,1,1,64]{3,2,1,0:T(1,128)}, u32[]{:S(2)}) copy-start(s32[1,1,1,64]{3,2,1,0:T(1,128)} %param.19) | copy-start | bytes 772
  7.2 29.1 %copy-start.11 = (s32[1,1,1,64]{3,2,1,0:T(1,128)S(1)}, s32[1,1,1,64]{3,2,1,0:T(1,128)}, u32[]{:S(2)}) copy-start(s32[1,1,1,64]{3,2,1,0:T(1,128)} %param.20) | copy-start | bytes 772
  7.2 44.5 %all-gather.5.cloned.1.call-start = ((), (), s32[]{:S(2)}) async-start(), calls=%async_computation.4 | async-start | bytes 2359296 | tf_op jit(solution)/shard_map/all_gather | solution.py:80
  9.0 97.3 %all-gather.7.cloned.1.call-start = ((), (), s32[]{:S(2)}) async-start(), calls=%async_computation.5 | async-start | bytes 2228224 | tf_op jit(solution)/shard_map/all_gather | solution.py:81
  12.1 14.0 %all-to-all-start.1 = ((s32[16,1,2]{2,1,0:T(1,128)}), s32[16,1,2]{2,1,0:T(1,128)S(1)}, u32[]{:S(2)}, u32[]{:S(2)}) async-start(s32[16,1,2]{2,1,0:T(1,128)} %copy.48), calls=%async_computation.1 | async-start | bytes 16384 | tf_op jit(solution)/shard_map/all_to_all | solution.py:51
  26.1 14.7 %all-to-all-start = ((s32[8,1,4]{2,1,0:T(1,128)}), s32[8,1,4]{2,1,0:T(1,128)S(1)}, u32[]{:S(2)}, u32[]{:S(2)}) async-start(s32[8,1,4]{2,1,0:T(1,128)} %copy.47), calls=%async_computation | async-start | bytes 8192 | tf_op jit(solution)/shard_map/all_to_all | solution.py:48
  34.3 201.6 %all-reduce.13.cloned.1.call-start = ((), (), s32[]{:S(2)}) async-start(), calls=%async_computation.10 | async-start | bytes 8388608
  55.4 53.4 %copy-start.9 = (s32[1,1,1,64,128]{4,3,2,1,0:T(8,128)S(1)}, s32[1,1,1,64,128]{4,3,2,1,0:T(8,128)}, u32[]{:S(2)}) copy-start(s32[1,1,1,64,128]{4,3,2,1,0:T(8,128)} %param.18) | copy-start | bytes 98308
  55.4 53.4 %copy-start.10 = (s32[1,1,1,64,128]{4,3,2,1,0:T(8,128)S(1)}, s32[1,1,1,64,128]{4,3,2,1,0:T(8,128)}, u32[]{:S(2)}) copy-start(s32[1,1,1,64,128]{4,3,2,1,0:T(8,128)} %param.17) | copy-start | bytes 98308
  108.9 4.1 copy-start.1
  113.0 1.4 copy-start.2
  122.1 171.6 %reduce-scatter.3.cloned.1.call-start = ((), (), s32[]{:S(2)}) async-start(), calls=%async_computation.6 | async-start | bytes 4718592 | tf_op jit(solution)/shard_map/reduce_scatter | solution.py:90
  132.3 1.0 copy-start.5
  132.3 2.2 copy-start.4
  132.3 3.9 copy-start.13
  132.3 372.9 %all-reduce.19.cloned.1.call-start = ((), (), s32[]{:S(2)}) async-start(), calls=%async_computation.13 | async-start | bytes 262144 | tf_op jit(solution)/shard_map/psum | solution.py:61
  136.1 405.1 %all-reduce.23.cloned.1.call-start = ((), (), s32[]{:S(2)}) async-start(), calls=%async_computation.15 | async-start | bytes 1572864 | tf_op jit(solution)/shard_map/psum | solution.py:92
  295.6 287.3 %all-gather.9.cloned.1.call-start = ((), (), s32[]{:S(2)}) async-start(), calls=%async_computation.7 | async-start | bytes 2359296 | tf_op jit(solution)/shard_map/all_gather | solution.py:80
  541.2 26.7 %copy-start.7 = (f32[128,512]{0,1:T(8,128)S(1)}, f32[128,512]{0,1:T(8,128)}, u32[]{:S(2)}) copy-start(f32[128,512]{0,1:T(8,128)} %get-tuple-element.18) | copy-start | bytes 786436
  544.4 92.8 %all-gather.11.cloned.1.call-start = ((), (), s32[]{:S(2)}) async-start(), calls=%async_computation.8 | async-start | bytes 2228224 | tf_op jit(solution)/shard_map/all_gather | solution.py:81
  569.5 281.0 %all-reduce.17.cloned.1.call-start = ((), (), s32[]{:S(2)}) async-start(), calls=%async_computation.12 | async-start | bytes 262144 | tf_op jit(solution)/shard_map/psum | solution.py:61
  571.8 397.6 %all-reduce.15.cloned.1.call-start = ((), (), s32[]{:S(2)}) async-start(), calls=%async_computation.11 | async-start | bytes 8388608
  639.7 4.1 copy-start
  643.9 1.4 copy-start.3
  652.9 374.5 %reduce-scatter.5.cloned.1.call-start = ((), (), s32[]{:S(2)}) async-start(), calls=%async_computation.9 | async-start | bytes 4718592 | tf_op jit(solution)/shard_map/reduce_scatter | solution.py:90
  663.0 400.3 %all-reduce.21.cloned.1.call-start = ((), (), s32[]{:S(2)}) async-start(), calls=%async_computation.14 | async-start | bytes 1572864 | tf_op jit(solution)/shard_map/psum | solution.py:92
  850.6 189.4 %copy-start.6 = (f32[128,128]{0,1:T(8,128)S(1)}, f32[128,128]{0,1:T(8,128)}, u32[]{:S(2)}) copy-start(f32[128,128]{0,1:T(8,128)} %get-tuple-element.12) | copy-start | bytes 196612
  1063.2 3.3 copy-start.8
Sparse Core Ops, SparseCore 0:
  10.4 41.2 all-gather.4
  54.7 51.5 all-gather.6
  122.2 113.6 all-reduce.12
  238.3 55.3 reduce-scatter.2
  299.1 206.1 all-reduce.18
  508.5 32.6 all-reduce.22
  544.5 38.3 all-gather.8
  585.9 51.1 all-gather.10
  642.7 207.7 all-reduce.16
  854.1 115.2 all-reduce.14
  972.1 55.3 reduce-scatter.4
  1030.7 29.7 all-reduce.20
where the time goes:
time: 1080 us
  waiting for transfers between devices  852 us (79%)
  other arithmetic  99.6 us (9%)
  matrix products  56.4 us (5%)
  local copies, waits for them, and re-layouts  34.4 us (3%)
  starting transfers between devices  17.6 us (2%)
  between operations  15.7 us (1%)
    psum x2, waiting for transfers between devices, on_device(): lax.psum((jnp.dot(users.T, users, precision=lax.Precision.HIGHEST, prefer...  396 us
    unnamed x14, waiting for transfers between devices  203 us
    reduce_scatter x2, waiting for transfers between devices, on_device(): lax.psum_scatter(user_pooled, 'tcol', scatter_dimension=0, tiled=True)  112 us
    all_gather x2, waiting for transfers between devices, on_device(): item_pool = lax.all_gather(item_half, 'trow', axis=0, tiled=True)  101 us
    another operation x12, other arithmetic, precondition(): factor = jnp.linalg.cholesky(gramian)  49.7 us
    another operation x8, other arithmetic, precondition(): return jax.scipy.linalg.cho_solve((factor, True), gradient.T).T  42.1 us
  transfers between devices with their start and end apart: 14, of which 13 were waited for; matrix products, arithmetic and copies ran while one was open for 15% of the time, Pallas kernels for 0%

commit v1 on v0

--- a/solution.py
+++ b/solution.py
@@ -58,22 +58,25 @@
     user_coef = 2.0 * all_items * own_users / (tile_size * tile_count * n_rep)
     item_coef = 2.0 * all_users * own_items / (tile_size * tile_count * n_rep)
     for iteration in range(ITERS):
-        gram_users, gram_items = lax.psum(
-            (
-                jnp.dot(
-                    users.T,
-                    users,
-                    precision=lax.Precision.HIGHEST,
-                    preferred_element_type=jnp.float32,
+        gram_users, gram_items = jax.lax.psum(
+            jax.lax.psum(
+                (
+                    jnp.dot(
+                        users.T,
+                        users,
+                        precision=lax.Precision.HIGHEST,
+                        preferred_element_type=jnp.float32,
+                    ),
+                    jnp.dot(
+                        items.T,
+                        items,
+                        precision=lax.Precision.HIGHEST,
+                        preferred_element_type=jnp.float32,
+                    ),
                 ),
-                jnp.dot(
-                    items.T,
-                    items,
-                    precision=lax.Precision.HIGHEST,
-                    preferred_element_type=jnp.float32,
-                ),
+                axis_name="tcol",
             ),
-            ("trow", "tcol"),
+            axis_name="trow",
         )
         user_half = users.astype(jnp.bfloat16).reshape(own_users, tile_size, rank_width)
         item_half = items.astype(jnp.bfloat16).reshape(own_items, tile_size, rank_width)

time: 1080 us -> 791 us (0.73)
  waiting for transfers between devices: 852 us -> 562 us
    unnamed x14 -> x12, waiting for transfers between devices: 203 us -> 0.2 us
    psum x2 -> x4, waiting for transfers between devices: 396 us -> 330 us  [the longest x2 222 us: on_device(): jax.lax.psum(jax.lax.psum((jnp.dot(users.T, users, precision=lax.Precisio...]
    reduce_scatter x2, waiting for transfers between devices: 112 us -> 97.3 us  [on_device(): lax.psum_scatter(user_pooled, 'tcol', scatter_dimension=0, tiled=True)]
  transfers between devices with their start and end apart: 14 -> 14, of which waited for: 13 -> 13; matrix products, arithmetic and copies ran while one was open for 15% -> 22% of each run, Pallas kernels for 0% -> 0%
where the time goes in v1:
time: 791 us; the launch traced here: 783 us
  waiting for transfers between devices  562 us (71%)
  other arithmetic  97.5 us (12%)
  matrix products  57.4 us (7%)
  local copies, waits for them, and re-layouts  32 us (4%)
  starting transfers between devices  17.6 us (2%)
  between operations  15.8 us (2%)
    psum x2, waiting for transfers between devices, on_device(): jax.lax.psum(jax.lax.psum((jnp.dot(users.T, users, precision=lax.Precisio...  222 us
    psum x2, waiting for transfers between devices, on_device(): jax.lax.psum((jnp.dot(users.T, users, precision=lax.Precision.HIGHEST, pr...  108 us
    all_gather x2, waiting for transfers between devices, on_device(): item_pool = lax.all_gather(item_half, 'trow', axis=0, tiled=True)  101 us
    reduce_scatter x2, waiting for transfers between devices, on_device(): lax.psum_scatter(user_pooled, 'tcol', scatter_dimension=0, tiled=True)  97.3 us
    another operation x12, other arithmetic, precondition(): factor = jnp.linalg.cholesky(gramian)  49.7 us
    another operation x8, other arithmetic, precondition(): return jax.scipy.linalg.cho_solve((factor, True), gradient.T).T  42 us
    all_gather x2, waiting for transfers between devices, on_device(): user_pool = lax.all_gather(user_half, 'tcol', axis=0, tiled=True)  20.2 us
    dot_general x4, matrix products, pool_sum(): jnp.dot(onehot, lower, preferred_element_type=jnp.float32)  19.5 us
  transfers between devices with their start and end apart: 14, of which 13 were waited for; matrix products, arithmetic and copies ran while one was open for 22% of the time, Pallas kernels for 0%

profile of v1, /device:TPU:1, one launch (start us, length us, event | category | flops | bytes accessed | tf_op | source)
XLA Modules:
  0.0 782.7 jit_solution(10044040879026775598)
XLA Ops:
  7.3 1.8 convert_element_type.69
  9.1 1.6 convert_element_type.70
  10.8 1.4 copy.48
  12.1 7.6 all-to-all-start.1
  19.8 2.3 fusion.58
  22.1 1.6 fusion.60
  24.5 1.7 all-to-all-done.1
  26.1 8.2 %all-to-all-start = ((s32[8,1,4]{2,1,0:T(1,128)}), s32[8,1,4]{2,1,0:T(1,128)S(1)}, u32[]{:S(2)}, u32[]{:S(2)}) async-start(s32[8,1,4]{2,1,0:T(1,128)} %copy.47), calls=%async_computation | async-start | bytes 8192 | tf_op jit(solution)/shard_map/all_to_all | solution.py:48
  35.6 0.8 gather_fusion.2
  36.5 4.5 all-to-all-done
  41.7 0.8 gather_fusion
  42.5 9.2 %all-gather.5.cloned.1.call-done = bf16[64,128,128]{2,1,0:T(8,128)(2,1)} async-done(((bf16[8,128,128]{2,1,0:T(8,128)(2,1)}), bf16[64,128,128]{2,1,0:T(8,128)(2,1)}) %all-gather.5.cloned.1.call-update) | async-done | bytes 2097168 | tf_op jit(solution)/shard_map/all_gather | solution.py:83
  51.7 3.8 gather_fusion.1
  55.5 50.7 %all-gather.7.cloned.1.call-done = bf16[64,128,128]{2,1,0:T(8,128)(2,1)} async-done(((bf16[4,128,128]{2,1,0:T(8,128)(2,1)}), bf16[64,128,128]{2,1,0:T(8,128)(2,1)}) %all-gather.7.cloned.1.call-update) | async-done | bytes 2097168 | tf_op jit(solution)/shard_map/all_gather | solution.py:84
  106.2 2.5 gather_fusion.3
  108.8 4.1 fusion.1
  112.9 0.9 fusion.61
  114.3 2.8 fusion.9
  117.1 4.9 convolution_add_fusion.2
  121.9 53.9 %all-reduce.21.cloned.1.call-done = (f32[128,128]{0,1:T(8,128)}, f32[128,128]{0,1:T(8,128)}) async-done(((f32[128,128]{0,1:T(8,128)}, f32[128,128]{0,1:T(8,128)}), (f32[128,128]{0,1:T(8,128)}, f32[128,128]{0,1:T(8,128)})) %all-reduce.21.cloned.1.call-update) | async-done | bytes 131088 | tf_op jit(solution)/shard_map/psum | solution.py:62
  176.1 2.3 fusion.59
  178.4 2.8 fusion.8
  181.2 4.9 convolution_add_fusion.3
  188.0 110.5 %all-reduce.17.cloned.1.call-done = (f32[128,128]{0,1:T(8,128)}, f32[64,16384]{1,0:T(8,128)}, f32[128,128]{0,1:T(8,128)}) async-done(((f32[128,128]{0,1:T(8,128)}, f32[64,16384]{1,0:T(8,128)}, f32[128,128]{0,1:T(8,128)}), (f32[128,128]{0,1:T(8,128)}, f32[64,16384]{1,0:T(8,128)}, f32[128,128]{0,1:T(8,128)})) %all-reduce.17.cloned.1.call-update) | async-done | bytes 4325392 | tf_op jit(solution)/shard_map/psum | solution.py:61
  298.5 1.1 constant_dynamic-slice_fusion.1
  299.6 0.9 reshape.383
  300.5 55.6 %reduce-scatter.3.cloned.1.call-done = f32[8,16384]{1,0:T(8,128)} async-done(((f32[64,16384]{1,0:T(8,128)}), f32[8,16384]{1,0:T(8,128)}) %reduce-scatter.3.cloned.1.call-update) | async-done | bytes 524304 | tf_op jit(solution)/shard_map/reduce_scatter | solution.py:93
  356.0 1.9 reshape.380
  358.7 11.7 %cholesky.74 = f32[128,128]{1,0:T(8,128)S(1)} custom-call(f32[128,128]{1,0:T(8,128)S(1)} %get-tuple-element.30), custom_call_target="Cholesky" | custom-call | tf_op jit(solution)/shard_map/jit(cholesky)/cholesky | solution.py:10
  371.8 9.8 %custom-call.14 = f32[1,128,128]{1,2,0:T(8,128)S(1)} custom-call(f32[1,128,128]{2,1,0:T(8,128)S(1)} %fusion.24), custom_call_target="InvertDiagBlocksLowerTriangular" | custom-call | tf_op jit(solution)/shard_map/jit(_cho_solve)/triangular_solve | solution.py:11
  381.6 6.9 all-reduce.25.cloned.1.call-done
  388.5 1.7 fusion.41
  390.9 0.8 copy.69
  392.4 11.7 %cholesky.85 = f32[128,128]{1,0:T(8,128)S(1)} custom-call(f32[128,128]{1,0:T(8,128)S(1)} %get-tuple-element.29), custom_call_target="Cholesky" | custom-call | tf_op jit(solution)/shard_map/jit(cholesky)/cholesky | solution.py:10
  405.4 9.8 %custom-call.15 = f32[1,128,128]{1,2,0:T(8,128)S(1)} custom-call(f32[1,128,128]{2,1,0:T(8,128)S(1)} %fusion.25), custom_call_target="InvertDiagBlocksLowerTriangular" | custom-call | tf_op jit(solution)/shard_map/jit(_cho_solve)/triangular_solve | solution.py:11
  416.1 0.8 copy.70
  416.9 1.0 fusion.62
  417.9 1.2 fusion.64
  419.4 11.0 %all-gather.9.cloned.1.call-done = bf16[64,128,128]{2,1,0:T(8,128)(2,1)} async-done(((bf16[8,128,128]{2,1,0:T(8,128)(2,1)}), bf16[64,128,128]{2,1,0:T(8,128)(2,1)}) %all-gather.9.cloned.1.call-update) | async-done | bytes 2097168 | tf_op jit(solution)/shard_map/all_gather | solution.py:83
  430.3 3.8 gather_fusion.4
  434.1 50.7 %all-gather.11.cloned.1.call-done = bf16[64,128,128]{2,1,0:T(8,128)(2,1)} async-done(((bf16[4,128,128]{2,1,0:T(8,128)(2,1)}), bf16[64,128,128]{2,1,0:T(8,128)(2,1)}) %all-gather.11.cloned.1.call-update) | async-done | bytes 2097168 | tf_op jit(solution)/shard_map/all_gather | solution.py:84
  484.8 2.5 gather_fusion.5
  487.3 4.1 fusion.3
  491.5 0.9 fusion.65
  492.9 2.8 fusion.11
  495.6 4.9 convolution_add_fusion
  500.5 54.0 %all-reduce.19.cloned.1.call-done = (f32[128,128]{0,1:T(8,128)}, f32[128,128]{0,1:T(8,128)}) async-done(((f32[128,128]{0,1:T(8,128)}, f32[128,128]{0,1:T(8,128)}), (f32[128,128]{0,1:T(8,128)}, f32[128,128]{0,1:T(8,128)})) %all-reduce.19.cloned.1.call-update) | async-done | bytes 131088 | tf_op jit(solution)/shard_map/psum | solution.py:62
  554.5 2.3 fusion.63
  556.8 2.8 fusion.10
  559.6 4.9 convolution_add_fusion.1
  564.8 111.9 %all-reduce.15.cloned.1.call-done = (f32[128,128]{0,1:T(8,128)}, f32[64,16384]{1,0:T(8,128)}, f32[128,128]{0,1:T(8,128)}) async-done(((f32[128,128]{0,1:T(8,128)}, f32[64,16384]{1,0:T(8,128)}, f32[128,128]{0,1:T(8,128)}), (f32[128,128]{0,1:T(8,128)}, f32[64,16384]{1,0:T(8,128)}, f32[128,128]{0,1:T(8,128)})) %all-reduce.15.cloned.1.call-update) | async-done | bytes 4325392 | tf_op jit(solution)/shard_map/psum | solution.py:61
  676.7 1.1 constant_dynamic-slice_fusion
  677.8 0.9 reshape.389
  678.7 0.9 copy.55
  679.6 0.9 fusion.35
  680.5 11.7 %cholesky.96 = f32[128,128]{1,0:T(8,128)S(1)} custom-call(f32[128,128]{1,0:T(8,128)S(1)} %fusion.35), custom_call_target="Cholesky" | custom-call | tf_op jit(solution)/shard_map/jit(cholesky)/cholesky | solution.py:10
  692.9 41.8 %reduce-scatter.5.cloned.1.call-done = f32[8,16384]{1,0:T(8,128)} async-done(((f32[64,16384]{1,0:T(8,128)}), f32[8,16384]{1,0:T(8,128)}) %reduce-scatter.5.cloned.1.call-update) | async-done | bytes 524304 | tf_op jit(solution)/shard_map/reduce_scatter | solution.py:93
  734.7 1.9 reshape.387
  737.3 9.8 %custom-call.16 = f32[1,128,128]{1,2,0:T(8,128)S(1)} custom-call(f32[1,128,128]{2,1,0:T(8,128)S(1)} %fusion.26), custom_call_target="InvertDiagBlocksLowerTriangular" | custom-call | tf_op jit(solution)/shard_map/jit(_cho_solve)/triangular_solve | solution.py:11
  747.2 11.7 %cholesky.107 = f32[128,128]{1,0:T(8,128)S(1)} custom-call(f32[128,128]{1,0:T(8,128)S(1)} %fusion.31), custom_call_target="Cholesky" | custom-call | tf_op jit(solution)/shard_map/jit(cholesky)/cholesky | solution.py:10
  760.3 10.0 %custom-call.17 = f32[1,128,128]{1,2,0:T(8,128)S(1)} custom-call(f32[1,128,128]{2,1,0:T(8,128)S(1)} %fusion.27), custom_call_target="InvertDiagBlocksLowerTriangular" | custom-call | tf_op jit(solution)/shard_map/jit(_cho_solve)/triangular_solve | solution.py:11
  770.4 1.7 fusion.33
  772.7 1.0 copy.61
  774.5 0.8 copy.62
  (101 shorter events, 15.9 us)
Async XLA Ops:
  7.2 14.9 %copy-start.4 = (f32[1024,128]{1,0:T(8,128)S(1)}, f32[1024,128]{1,0:T(8,128)}, u32[]{:S(2)}) copy-start(f32[1024,128]{1,0:T(8,128)} %param.14) | copy-start | bytes 1572868
  7.2 16.5 %copy-start.15 = (s32[1,1,1,64]{3,2,1,0:T(1,128)S(1)}, s32[1,1,1,64]{3,2,1,0:T(1,128)}, u32[]{:S(2)}) copy-start(s32[1,1,1,64]{3,2,1,0:T(1,128)} %param.19) | copy-start | bytes 772
  7.2 16.6 %copy-start.14 = (s32[1,1,1,64]{3,2,1,0:T(1,128)S(1)}, s32[1,1,1,64]{3,2,1,0:T(1,128)}, u32[]{:S(2)}) copy-start(s32[1,1,1,64]{3,2,1,0:T(1,128)} %param.20) | copy-start | bytes 772
  7.2 16.6 %copy-start.13 = (s32[1,1,1,8,4]{3,4,2,1,0:T(4,128)S(1)}, s32[1,1,1,8,4]{3,4,2,1,0:T(4,128)}, u32[]{:S(2)}) copy-start(s32[1,1,1,8,4]{3,4,2,1,0:T(4,128)} %param.21) | copy-start | bytes 388
  7.2 44.5 %all-gather.5.cloned.1.call-start = ((), (), s32[]{:S(2)}) async-start(), calls=%async_computation.4 | async-start | bytes 2359296 | tf_op jit(solution)/shard_map/all_gather | solution.py:83
  9.1 97.1 %all-gather.7.cloned.1.call-start = ((), (), s32[]{:S(2)}) async-start(), calls=%async_computation.5 | async-start | bytes 2228224 | tf_op jit(solution)/shard_map/all_gather | solution.py:84
  12.1 14.0 %all-to-all-start.1 = ((s32[16,1,2]{2,1,0:T(1,128)}), s32[16,1,2]{2,1,0:T(1,128)S(1)}, u32[]{:S(2)}, u32[]{:S(2)}) async-start(s32[16,1,2]{2,1,0:T(1,128)} %copy.48), calls=%async_computation.1 | async-start | bytes 16384 | tf_op jit(solution)/shard_map/all_to_all | solution.py:51
  19.7 156.1 %all-reduce.21.cloned.1.call-start = ((), (), s32[]{:S(2)}) async-start(), calls=%async_computation.13 | async-start | bytes 262144 | tf_op jit(solution)/shard_map/psum | solution.py:62
  26.1 14.8 %all-to-all-start = ((s32[8,1,4]{2,1,0:T(1,128)}), s32[8,1,4]{2,1,0:T(1,128)S(1)}, u32[]{:S(2)}, u32[]{:S(2)}) async-start(s32[8,1,4]{2,1,0:T(1,128)} %copy.47), calls=%async_computation | async-start | bytes 8192 | tf_op jit(solution)/shard_map/all_to_all | solution.py:48
  34.3 264.1 %all-reduce.17.cloned.1.call-start = ((), (), s32[]{:S(2)}) async-start(), calls=%async_computation.11 | async-start | bytes 8650752 | tf_op jit(solution)/shard_map/psum | solution.py:61
  55.5 53.3 %copy-start.11 = (s32[1,1,1,64,128]{4,3,2,1,0:T(8,128)S(1)}, s32[1,1,1,64,128]{4,3,2,1,0:T(8,128)}, u32[]{:S(2)}) copy-start(s32[1,1,1,64,128]{4,3,2,1,0:T(8,128)} %param.18) | copy-start | bytes 98308
  55.5 53.3 %copy-start.12 = (s32[1,1,1,64,128]{4,3,2,1,0:T(8,128)S(1)}, s32[1,1,1,64,128]{4,3,2,1,0:T(8,128)}, u32[]{:S(2)}) copy-start(s32[1,1,1,64,128]{4,3,2,1,0:T(8,128)} %param.17) | copy-start | bytes 98308
  108.8 4.1 copy-start.1
  112.9 1.4 copy-start.2
  175.8 180.2 %reduce-scatter.3.cloned.1.call-start = ((), (), s32[]{:S(2)}) async-start(), calls=%async_computation.6 | async-start | bytes 4718592 | tf_op jit(solution)/shard_map/reduce_scatter | solution.py:93
  186.0 0.7 copy-start.16
  186.1 202.5 %all-reduce.25.cloned.1.call-start = ((), (), s32[]{:S(2)}) async-start(), calls=%async_computation.15 | async-start | bytes 1572864 | tf_op jit(solution)/shard_map/psum | solution.py:95
  298.4 60.0 %copy-start.10 = (f32[128,128]{0,1:T(8,128)S(1)}, f32[128,128]{0,1:T(8,128)}, u32[]{:S(2)}) copy-start(f32[128,128]{0,1:T(8,128)} %get-tuple-element.16) | copy-start | bytes 196612
  298.4 60.1 %copy-start.9 = (f32[128,128]{0,1:T(8,128)S(1)}, f32[128,128]{0,1:T(8,128)}, u32[]{:S(2)}) copy-start(f32[128,128]{0,1:T(8,128)} %get-tuple-element.14) | copy-start | bytes 196612
  358.0 72.4 %all-gather.9.cloned.1.call-start = ((), (), s32[]{:S(2)}) async-start(), calls=%async_computation.7 | async-start | bytes 2359296 | tf_op jit(solution)/shard_map/all_gather | solution.py:83
  358.7 33.5 %copy-start.5 = (f32[512,128]{1,0:T(8,128)S(1)}, f32[512,128]{1,0:T(8,128)}, u32[]{:S(2)}) copy-start(f32[512,128]{1,0:T(8,128)} %param.15) | copy-start | bytes 786436
  388.5 26.7 %copy-start.7 = (f32[128,512]{0,1:T(8,128)S(1)}, f32[128,512]{0,1:T(8,128)}, u32[]{:S(2)}) copy-start(f32[128,512]{0,1:T(8,128)} %get-tuple-element.24) | copy-start | bytes 786436
  391.7 93.0 %all-gather.11.cloned.1.call-start = ((), (), s32[]{:S(2)}) async-start(), calls=%async_computation.8 | async-start | bytes 2228224 | tf_op jit(solution)/shard_map/all_gather | solution.py:84
  416.9 137.6 %all-reduce.19.cloned.1.call-start = ((), (), s32[]{:S(2)}) async-start(), calls=%async_computation.12 | async-start | bytes 262144 | tf_op jit(solution)/shard_map/psum | solution.py:62
  419.1 257.6 %all-reduce.15.cloned.1.call-start = ((), (), s32[]{:S(2)}) async-start(), calls=%async_computation.10 | async-start | bytes 8650752 | tf_op jit(solution)/shard_map/psum | solution.py:61
  487.3 4.1 copy-start
  491.5 1.4 copy-start.3
  554.5 180.2 %reduce-scatter.5.cloned.1.call-start = ((), (), s32[]{:S(2)}) async-start(), calls=%async_computation.9 | async-start | bytes 4718592 | tf_op jit(solution)/shard_map/reduce_scatter | solution.py:93
  564.5 205.9 %all-reduce.23.cloned.1.call-start = ((), (), s32[]{:S(2)}) async-start(), calls=%async_computation.14 | async-start | bytes 1572864 | tf_op jit(solution)/shard_map/psum | solution.py:95
  676.7 70.4 %copy-start.6 = (f32[128,128]{0,1:T(8,128)S(1)}, f32[128,128]{0,1:T(8,128)}, u32[]{:S(2)}) copy-start(f32[128,128]{0,1:T(8,128)} %get-tuple-element.13) | copy-start | bytes 196612
  770.4 3.3 copy-start.8
Sparse Core Ops, SparseCore 0:
  10.4 41.2 all-gather.4
  54.7 51.4 all-gather.6
  108.5 67.2 all-reduce.20
  179.7 118.6 all-reduce.16
  300.8 55.1 reduce-scatter.2
  359.1 29.3 all-reduce.24
  391.8 38.4 all-gather.8
  433.6 51.1 all-gather.10
  487.2 67.1 all-reduce.18
  558.0 118.6 all-reduce.14
  679.4 55.2 reduce-scatter.4
  738.0 29.5 all-reduce.22
